TPU v7x, 512 devices: a whole 4x8x8 slice. The times are simulated.
512 devices in a mesh: scen: 8 (over x, core), bus: 64 (over y, z).
Axes of the slice: x: 4, y: 8, z: 8, core: 2. Of those that a mesh axis runs over, the one named last changes fastest.
Arguments:
- injections: bfloat16 [1024, 16384], P(('scen', 'bus')), may hold values from -6 to 6
- tile_values: bfloat16 [4096, 128, 128], P('bus', 'scen'), may hold values from -0.109375 to 0.109375
- tile_line: int32 [4096], P('bus'), may hold values from 0 to 191, as said below
- tile_bus: int32 [4096], P('bus'), may hold values from 0 to 1
- flow_pred: bfloat16 [1024, 24576], P('scen', 'bus'), may hold values from -6 to 6
- line_limit: int32 [24576], P('bus'), may hold values from 50 to 199
Outputs:
- grad_injections: bfloat16 [1024, 16384], P(('scen', 'bus'))
- flows: float32 [1024, 24576], P('scen', 'bus')
Inputs may be any that keep to these rules, and one draw needn't show every extreme that they name: `tile_line`: tile t is held by bus index t // 64; line block b is owned by bus index b // 3. Of the 64 tiles of one bus index at most 2 have line blocks of one owner, and in every draw some owner gets exactly 2 tiles from every bus index. A pair of line block and bus block may occur in several tiles; their values add.
All inputs are finite; a program needn't handle non-finite values.
Results may differ from a plain program's by a relative error of at most 0.0039.
Values may be sent and summed in bfloat16 or wider, within the bound.
No kernel may reach another device: no remote copies, remote signals or barrier semaphores. Data moves between devices by JAX's collectives and lax.ppermute only.
A program may use at most 64 MiB of HBM per device.

v0:
```python
import jax
import jax.numpy as jnp
from jax import lax
from jax.sharding import PartitionSpec as P


def per_device(injections, tile_values, tile_line, tile_bus, flow_pred, line_limit):
    bus_count = lax.axis_size("bus")
    local_inj = lax.all_to_all(injections, "bus", split_axis=1, concat_axis=0, tiled=True)
    tile_full = lax.all_gather(tile_values, "scen", axis=1, tiled=True)
    tile_count = tile_full.shape[0]
    tile_size = tile_full.shape[1]
    row_count = local_inj.shape[0]
    blocks_here = local_inj.shape[1] // tile_size
    line_blocks = flow_pred.shape[1] // tile_size
    per_owner = tile_count // bus_count
    capacity = per_owner + max(1, tile_count // (2 * bus_count))
    slot_total = bus_count * capacity
    inj_blocks = local_inj.reshape(row_count, blocks_here, tile_size)
    per_tile_inj = jnp.take(inj_blocks, tile_bus, axis=1)
    partial_flows = jnp.einsum(
        "stb,tlb->tsl", per_tile_inj, tile_full, preferred_element_type=jnp.float32
    )
    owner_index = tile_line // line_blocks
    within_owner = tile_line % line_blocks
    owner_hits = (owner_index[:, None] == jnp.arange(bus_count, dtype=jnp.int32)[None, :]).astype(
        jnp.int32
    )
    rank_within = jnp.sum(jnp.cumsum(owner_hits, axis=0) * owner_hits, axis=1) - 1
    slot_index = owner_index * capacity + rank_within
    send_buffer = (
        jnp.zeros((slot_total, row_count, tile_size), jnp.float32).at[slot_index].set(partial_flows)
    )
    slot_label = jnp.full((slot_total,), -1, jnp.int32).at[slot_index].set(within_owner)
    received, received_label = (
        lax.all_to_all(send_buffer, "bus", split_axis=0, concat_axis=0, tiled=True),
        lax.all_to_all(slot_label, "bus", split_axis=0, concat_axis=0, tiled=True),
    )
    select_mask = (
        received_label[None, :] == jnp.arange(line_blocks, dtype=jnp.int32)[:, None]
    ).astype(jnp.float32)
    flow_blocks = jnp.einsum("ms,srl->rml", select_mask, received, precision=lax.Precision.HIGHEST)
    flows = flow_blocks.reshape(row_count, line_blocks * tile_size)
    line_cap = line_limit.astype(jnp.float32) * 0.01
    residual = flows - flow_pred.astype(jnp.float32)
    grad_flow = (
        residual
        + jax.nn.sigmoid(4.0 * (flows - line_cap))
        - jax.nn.sigmoid(4.0 * (-flows - line_cap))
    ).astype(jnp.bfloat16)
    gathered = lax.all_gather(grad_flow, "bus", axis=1, tiled=True)
    gathered_blocks = gathered.reshape(row_count, gathered.shape[1] // tile_size, tile_size)
    per_tile_grad = jnp.take(gathered_blocks, tile_line, axis=1)
    contrib = jnp.einsum(
        "stl,tlb->stb", per_tile_grad, tile_full, preferred_element_type=jnp.float32
    )
    bus_select = (tile_bus[:, None] == jnp.arange(blocks_here, dtype=jnp.int32)[None, :]).astype(
        jnp.float32
    )
    grad_blocks_bus = jnp.einsum(
        "stb,tk->skb", contrib, bus_select, precision=lax.Precision.HIGHEST
    )
    grad_local = grad_blocks_bus.reshape(row_count, blocks_here * tile_size).astype(jnp.bfloat16)
    grad_injections = lax.all_to_all(grad_local, "bus", split_axis=0, concat_axis=1, tiled=True)
    return (grad_injections, flows)


def solution(mesh):
    return jax.shard_map(
        per_device,
        mesh=mesh,
        in_specs=(
            P(("scen", "bus"), None),
            P("bus", "scen", None),
            P("bus"),
            P("bus"),
            P("scen", "bus"),
            P("bus"),
        ),
        out_specs=(P(("scen", "bus"), None), P("scen", "bus")),
        check_vma=False,
    )
```

profile of v0, /device:TPU:2, one launch (start us, length us, event | category | flops | bytes accessed | tf_op | source)
XLA Modules:
  0.0 535.0 jit_solution(14193557377811817124)
XLA Ops:
  7.2 0.7 all-gather.3.cloned.1.call-update
  7.9 16.6 %all-to-all-start = ((bf16[2,64,256]{2,0,1:T(2,128)(2,1)}), bf16[2,64,256]{2,0,1:T(2,128)(2,1)S(1)}, u32[]{:S(2)}, u32[]{:S(2)}) async-start(bf16[2,64,256]{2,0,1:T(2,128)(2,1)} %bitcast.34), calls=%async_computation | async-start | bytes 131072 | tf_op jit(solution)/shard_map/all_to_all | solution.py:9
  26.9 0.8 scatter_custom_fusion.1
  27.6 0.8 all_to_all.37
  28.4 8.4 %all-to-all-done = bf16[2,64,256]{2,0,1:T(2,128)(2,1)S(1)} async-done(((bf16[2,64,256]{2,0,1:T(2,128)(2,1)}), bf16[2,64,256]{2,0,1:T(2,128)(2,1)S(1)}, u32[]{:S(2)}, u32[]{:S(2)}) %all-to-all-start) | async-done | bytes 65568 | tf_op jit(solution)/shard_map/all_to_all | solution.py:9
  36.8 4.6 all-to-all-start.2
  41.4 1.0 gather_fusion
  42.4 4.4 all-gather.3.cloned.1.call-done
  46.9 5.2 fusion.5
  52.0 4.3 broadcast_in_dim.41
  56.3 12.0 %scatter_fusion = f32[128,128,128]{2,1,0:T(8,128)} fusion(f32[128,128,128]{2,1,0:T(8,128)} %broadcast_in_dim.41, s32[64]{0:T(128)S(1)} %compare_select_fusion.1, f32[64,128,128]{2,1,0:T(8,128)} %fusion.5), kind=kCustom, calls=%fused_computation.2 | custom fusion | bytes 12583168 | tf_op jit(solution)/shard_map/scatter | solution.py:32
  68.4 13.8 %all-to-all-start.1 = ((f32[128,128,128]{2,1,0:T(8,128)}), f32[128,128,128]{2,1,0:T(8,128)}, u32[]{:S(2)}, u32[]{:S(2)}) async-start(f32[128,128,128]{2,1,0:T(8,128)} %scatter_fusion), calls=%async_computation.1 | async-start | bytes 16777216 | tf_op jit(solution)/shard_map/all_to_all | solution.py:36
  83.0 0.7 reduce.3
  83.9 234.9 %all-to-all-done.1 = f32[128,128,128]{2,1,0:T(8,128)} async-done(((f32[128,128,128]{2,1,0:T(8,128)}), f32[128,128,128]{2,1,0:T(8,128)}, u32[]{:S(2)}, u32[]{:S(2)}) %all-to-all-start.1) | async-done | bytes 8388640 | tf_op jit(solution)/shard_map/all_to_all | solution.py:36
  318.8 10.4 %fusion.11 = f32[128,3,128]{2,1,0:T(4,128)S(1)} fusion(f32[128,128,128]{2,1,0:T(8,128)} %all-to-all-done.1, s32[128]{0:T(128)S(1)} %eq.49), kind=kOutput, calls=%fused_computation.16 | convolution fusion | flops 75497856 | bytes 8585728 | tf_op jit(solution)/shard_map/ms,srl->rml/dot_general | solution.py:42
  329.4 0.8 subtract_convert_fusion
  330.3 157.1 %all-gather.5.cloned.1.call-done = bf16[128,24576]{0,1:T(8,128)(2,1)} async-done(((bf16[128,384]{0,1:T(8,128)(2,1)}), bf16[128,24576]{0,1:T(8,128)(2,1)}) %all-gather.5.cloned.1.call-update) | async-done | bytes 6291472 | tf_op jit(solution)/shard_map/all_gather | solution.py:51
  487.4 8.7 %copy.31 = bf16[128,192,128]{2,0,1:T(8,128)(2,1)} copy(bf16[128,192,128]{0,2,1:T(8,128)(2,1)} %bitcast.30) | data formatting | bytes 12582912 | tf_op jit(solution)/shard_map/reshape | solution.py:52
  496.0 3.7 gather_fusion.1
  499.8 2.4 convolution_bitcast_fusion
  502.1 3.8 fusion.17
  506.6 8.6 %all-to-all-start.3 = ((bf16[64,2,256]{2,1,0:T(2,128)(2,1)}), bf16[64,2,256]{2,1,0:T(2,128)(2,1)S(1)}, u32[]{:S(2)}, u32[]{:S(2)}) async-start(bf16[64,2,256]{2,1,0:T(2,128)(2,1)} %convert_element_type.30), calls=%async_computation.3 | async-start | bytes 131072 | tf_op jit(solution)/shard_map/all_to_all | solution.py:64
  515.2 0.8 copy.34
  516.0 11.5 %all-to-all-done.3 = bf16[64,2,256]{2,1,0:T(2,128)(2,1)S(1)} async-done(((bf16[64,2,256]{2,1,0:T(2,128)(2,1)}), bf16[64,2,256]{2,1,0:T(2,128)(2,1)S(1)}, u32[]{:S(2)}, u32[]{:S(2)}) %all-to-all-start.3) | async-done | bytes 65568 | tf_op jit(solution)/shard_map/all_to_all | solution.py:64
  (31 shorter events, 4.9 us)
Async XLA Ops:
  7.2 39.7 %all-gather.3.cloned.1.call-start = ((), (), s32[]{:S(2)}) async-start(), calls=%async_computation.4 | async-start | bytes 2359296 | tf_op jit(solution)/shard_map/all_gather | solution.py:10
  7.9 28.9 %all-to-all-start = ((bf16[2,64,256]{2,0,1:T(2,128)(2,1)}), bf16[2,64,256]{2,0,1:T(2,128)(2,1)S(1)}, u32[]{:S(2)}, u32[]{:S(2)}) async-start(bf16[2,64,256]{2,0,1:T(2,128)(2,1)} %bitcast.34), calls=%async_computation | async-start | bytes 131072 | tf_op jit(solution)/shard_map/all_to_all | solution.py:9
  36.8 31.6 %all-to-all-start.2 = ((s32[64,2,1]{1,2,0:T(1,128)}), s32[64,2,1]{1,2,0:T(1,128)S(1)}, u32[]{:S(2)}, u32[]{:S(2)}) async-start(s32[64,2,1]{1,2,0:T(1,128)} %bitcast.4), calls=%async_computation.2 | async-start | bytes 65536 | tf_op jit(solution)/shard_map/all_to_all | solution.py:37
  68.3 14.0 %copy-start = (bf16[128,384]{1,0:T(8,128)(2,1)S(1)}, bf16[128,384]{1,0:T(8,128)(2,1)}, u32[]{:S(2)}) copy-start(bf16[128,384]{1,0:T(8,128)(2,1)} %param.10) | copy-start | bytes 294916
  68.3 14.1 %copy-start.1 = (s32[384]{0:T(512)S(1)}, s32[384]{0:T(512)}, u32[]{:S(2)}) copy-start(s32[384]{0:T(512)} %param.11) | copy-start | bytes 4612
  68.4 250.5 %all-to-all-start.1 = ((f32[128,128,128]{2,1,0:T(8,128)}), f32[128,128,128]{2,1,0:T(8,128)}, u32[]{:S(2)}, u32[]{:S(2)}) async-start(f32[128,128,128]{2,1,0:T(8,128)} %scatter_fusion), calls=%async_computation.1 | async-start | bytes 16777216 | tf_op jit(solution)/shard_map/all_to_all | solution.py:36
  82.1 405.2 %all-gather.5.cloned.1.call-start = ((), (), s32[]{:S(2)}) async-start(), calls=%async_computation.5 | async-start | bytes 6389760 | tf_op jit(solution)/shard_map/all_gather | solution.py:51
  83.9 246.4 %copy-start.3 = (s32[64]{0:T(128)S(1)}, s32[64]{0:T(128)}, u32[]{:S(2)}) copy-start(s32[64]{0:T(128)} %param.8) | copy-start | bytes 772
  499.8 2.4 copy-start.2
  506.6 20.9 %all-to-all-start.3 = ((bf16[64,2,256]{2,1,0:T(2,128)(2,1)}), bf16[64,2,256]{2,1,0:T(2,128)(2,1)S(1)}, u32[]{:S(2)}, u32[]{:S(2)}) async-start(bf16[64,2,256]{2,1,0:T(2,128)(2,1)} %convert_element_type.30), calls=%async_computation.3 | async-start | bytes 131072 | tf_op jit(solution)/shard_map/all_to_all | solution.py:64
Sparse Core Ops, SparseCore 0:
  10.1 36.6 all-gather.2
  330.4 156.9 all-gather.4
where the time goes:
time: 536 us; the launch traced here: 535 us
  waiting for transfers between devices  417 us (78%)
  starting transfers between devices  43.8 us (8%)
  local copies, waits for them, and re-layouts  34.3 us (6%)
  matrix products  21.8 us (4%)
  between operations  14.2 us (3%)
    all_to_all x1, waiting for transfers between devices, per_device(): lax.all_to_all(send_buffer, 'bus', split_axis=0, concat_axis=0, tiled=True)  235 us
    all_gather x1, waiting for transfers between devices, per_device(): gathered = lax.all_gather(grad_flow, 'bus', axis=1, tiled=True)  157 us
    all_to_all x1, starting transfers between devices, per_device(): lax.all_to_all(injections, 'bus', split_axis=1, concat_axis=0, tiled=True)  16.6 us
    all_to_all x1, starting transfers between devices, per_device(): lax.all_to_all(send_buffer, 'bus', split_axis=0, concat_axis=0, tiled=True)  13.8 us
    scatter x1, local copies, waits for them, and re-layouts, per_device(): jnp.zeros((slot_total, row_count, tile_size), jnp.float32).at[slot_index]  12 us
    all_to_all x1, waiting for transfers between devices, per_device(): lax.all_to_all(grad_local, 'bus', split_axis=0, concat_axis=1, tiled=True)  11.5 us
  transfers between devices with their start and end apart: 6, of which 5 were waited for; matrix products, arithmetic and copies ran while one was open for 5% of the time, Pallas kernels for 0%

commit v1 on v0

--- a/solution.py
+++ b/solution.py
@@ -2,6 +2,7 @@
 import jax.numpy as jnp
 from jax import lax
 from jax.sharding import PartitionSpec as P
+from jax.lax import all_to_all, axis_size
 
 
 def per_device(injections, tile_values, tile_line, tile_bus, flow_pred, line_limit):
@@ -48,7 +49,9 @@
         + jax.nn.sigmoid(4.0 * (flows - line_cap))
         - jax.nn.sigmoid(4.0 * (-flows - line_cap))
     ).astype(jnp.bfloat16)
-    gathered = lax.all_gather(grad_flow, "bus", axis=1, tiled=True)
+    gathered = jnp.concatenate(
+        all_to_all(jnp.stack([grad_flow] * axis_size("bus"), axis=0), "bus", 0, 0), 1
+    )
     gathered_blocks = gathered.reshape(row_count, gathered.shape[1] // tile_size, tile_size)
     per_tile_grad = jnp.take(gathered_blocks, tile_line, axis=1)
     contrib = jnp.einsum(

time: 536 us -> 658 us (1.23)
  the two profiles are of different devices: /device:TPU:2 before, /device:TPU:8 now
where the time goes in v1:
time: 658 us; the launch traced here: 657 us
  waiting for transfers between devices  462 us (70%)
  starting transfers between devices  117 us (18%)
  local copies, waits for them, and re-layouts  38.3 us (6%)
  matrix products  21.7 us (3%)
  between operations  14.2 us (2%)
    all_to_all x1, waiting for transfers between devices, per_device(): lax.all_to_all(send_buffer, 'bus', split_axis=0, concat_axis=0, tiled=True)  250 us
    all_to_all x1, waiting for transfers between devices, per_device(): all_to_all(jnp.stack([grad_flow] * axis_size('bus'), axis=0), 'bus', 0, 0)  188 us
    all_to_all x1, starting transfers between devices, per_device(): all_to_all(jnp.stack([grad_flow] * axis_size('bus'), axis=0), 'bus', 0, 0)  49.9 us
    all_to_all x1, starting transfers between devices, per_device(): lax.all_to_all(grad_local, 'bus', split_axis=0, concat_axis=1, tiled=True)  31.7 us
    all_to_all x1, starting transfers between devices, per_device(): lax.all_to_all(injections, 'bus', split_axis=1, concat_axis=0, tiled=True)  16.6 us
    all_to_all x1, starting transfers between devices, per_device(): lax.all_to_all(send_buffer, 'bus', split_axis=0, concat_axis=0, tiled=True)  13.8 us
  transfers between devices with their start and end apart: 6, of which 5 were waited for; matrix products, arithmetic and copies ran while one was open for 4% of the time, Pallas kernels for 0%

profile of v1, /device:TPU:8, one launch (start us, length us, event | category | flops | bytes accessed | tf_op | source)
XLA Modules:
  0.0 656.7 jit_solution(9815568015619625779)
XLA Ops:
  7.9 16.6 %all-to-all-start = ((bf16[2,64,256]{2,0,1:T(2,128)(2,1)}), bf16[2,64,256]{2,0,1:T(2,128)(2,1)S(1)}, u32[]{:S(2)}, u32[]{:S(2)}) async-start(bf16[2,64,256]{2,0,1:T(2,128)(2,1)} %bitcast.35), calls=%async_computation | async-start | bytes 131072 | tf_op jit(solution)/shard_map/all_to_all | solution.py:10
  26.9 0.8 scatter_custom_fusion.1
  27.6 0.8 all_to_all.40
  28.4 7.5 %all-to-all-done = bf16[2,64,256]{2,0,1:T(2,128)(2,1)S(1)} async-done(((bf16[2,64,256]{2,0,1:T(2,128)(2,1)}), bf16[2,64,256]{2,0,1:T(2,128)(2,1)S(1)}, u32[]{:S(2)}, u32[]{:S(2)}) %all-to-all-start) | async-done | bytes 65568 | tf_op jit(solution)/shard_map/all_to_all | solution.py:10
  35.9 5.4 all-to-all-start.2
  41.4 1.0 gather_fusion
  42.3 4.9 all-gather.2.cloned.1.call-done
  47.2 5.2 fusion.5
  52.4 4.3 broadcast_in_dim.41
  56.7 11.9 %scatter_fusion = f32[128,128,128]{2,1,0:T(8,128)} fusion(f32[128,128,128]{2,1,0:T(8,128)} %broadcast_in_dim.41, s32[64]{0:T(128)S(1)} %compare_select_fusion.1, f32[64,128,128]{2,1,0:T(8,128)} %fusion.5), kind=kCustom, calls=%fused_computation.2 | custom fusion | bytes 12583168 | tf_op jit(solution)/shard_map/scatter | solution.py:33
  68.6 13.8 %all-to-all-start.1 = ((f32[128,128,128]{2,1,0:T(8,128)}), f32[128,128,128]{2,1,0:T(8,128)}, u32[]{:S(2)}, u32[]{:S(2)}) async-start(f32[128,128,128]{2,1,0:T(8,128)} %scatter_fusion), calls=%async_computation.1 | async-start | bytes 16777216 | tf_op jit(solution)/shard_map/all_to_all | solution.py:37
  83.1 0.7 reduce.3
  84.0 250.0 %all-to-all-done.1 = f32[128,128,128]{2,1,0:T(8,128)} async-done(((f32[128,128,128]{2,1,0:T(8,128)}), f32[128,128,128]{2,1,0:T(8,128)}, u32[]{:S(2)}, u32[]{:S(2)}) %all-to-all-start.1) | async-done | bytes 8388640 | tf_op jit(solution)/shard_map/all_to_all | solution.py:37
  334.0 10.4 %fusion.11 = f32[128,3,128]{2,1,0:T(4,128)S(1)} fusion(f32[128,128,128]{2,1,0:T(8,128)} %all-to-all-done.1, s32[128]{0:T(128)S(1)} %eq.49), kind=kOutput, calls=%fused_computation.16 | convolution fusion | flops 75497856 | bytes 8585728 | tf_op jit(solution)/shard_map/ms,srl->rml/dot_general | solution.py:43
  344.8 4.2 stack.2
  349.0 49.9 %all-to-all-start.3 = ((bf16[64,128,384]{1,2,0:T(8,128)(2,1)}), bf16[64,128,384]{1,2,0:T(8,128)(2,1)}, u32[]{:S(2)}, u32[]{:S(2)}) async-start(bf16[64,128,384]{1,2,0:T(8,128)(2,1)} %stack.2), calls=%async_computation.3 | async-start | bytes 12582912 | tf_op jit(solution)/shard_map/all_to_all | solution.py:53
  398.9 188.0 %all-to-all-done.3 = bf16[64,128,384]{1,2,0:T(8,128)(2,1)} async-done(((bf16[64,128,384]{1,2,0:T(8,128)(2,1)}), bf16[64,128,384]{1,2,0:T(8,128)(2,1)}, u32[]{:S(2)}, u32[]{:S(2)}) %all-to-all-start.3) | async-done | bytes 6291488 | tf_op jit(solution)/shard_map/all_to_all | solution.py:53
  586.8 8.6 %copy.23 = bf16[128,192,128]{2,0,1:T(8,128)(2,1)} copy(bf16[128,192,128]{0,2,1:T(8,128)(2,1)} %bitcast.9) | data formatting | bytes 12582912 | tf_op jit(solution)/shard_map/reshape;reshape | solution.py:55
  595.4 3.7 gather_fusion.1
  599.2 2.4 convolution_bitcast_fusion
  601.6 3.8 fusion.17
  606.1 31.7 %all-to-all-start.4 = ((bf16[64,2,256]{2,1,0:T(2,128)(2,1)}), bf16[64,2,256]{2,1,0:T(2,128)(2,1)S(1)}, u32[]{:S(2)}, u32[]{:S(2)}) async-start(bf16[64,2,256]{2,1,0:T(2,128)(2,1)} %convert_element_type.30), calls=%async_computation.4 | async-start | bytes 131072 | tf_op jit(solution)/shard_map/all_to_all | solution.py:67
  637.8 0.8 copy.26
  638.6 10.6 %all-to-all-done.4 = bf16[64,2,256]{2,1,0:T(2,128)(2,1)S(1)} async-done(((bf16[64,2,256]{2,1,0:T(2,128)(2,1)}), bf16[64,2,256]{2,1,0:T(2,128)(2,1)S(1)}, u32[]{:S(2)}, u32[]{:S(2)}) %all-to-all-start.4) | async-done | bytes 65568 | tf_op jit(solution)/shard_map/all_to_all | solution.py:67
  (31 shorter events, 5.6 us)
Async XLA Ops:
  7.2 40.1 %all-gather.2.cloned.1.call-start = ((), (), s32[]{:S(2)}) async-start(), calls=%async_computation.5 | async-start | bytes 2359296 | tf_op jit(solution)/shard_map/all_gather | solution.py:11
  7.9 28.0 %all-to-all-start = ((bf16[2,64,256]{2,0,1:T(2,128)(2,1)}), bf16[2,64,256]{2,0,1:T(2,128)(2,1)S(1)}, u32[]{:S(2)}, u32[]{:S(2)}) async-start(bf16[2,64,256]{2,0,1:T(2,128)(2,1)} %bitcast.35), calls=%async_computation | async-start | bytes 131072 | tf_op jit(solution)/shard_map/all_to_all | solution.py:10
  35.9 32.7 %all-to-all-start.2 = ((s32[64,2,1]{1,2,0:T(1,128)}), s32[64,2,1]{1,2,0:T(1,128)S(1)}, u32[]{:S(2)}, u32[]{:S(2)}) async-start(s32[64,2,1]{1,2,0:T(1,128)} %bitcast.4), calls=%async_computation.2 | async-start | bytes 65536 | tf_op jit(solution)/shard_map/all_to_all | solution.py:38
  68.6 13.8 %copy-start = (bf16[128,384]{1,0:T(8,128)(2,1)S(1)}, bf16[128,384]{1,0:T(8,128)(2,1)}, u32[]{:S(2)}) copy-start(bf16[128,384]{1,0:T(8,128)(2,1)} %param.10) | copy-start | bytes 294916
  68.6 14.0 %copy-start.1 = (s32[384]{0:T(512)S(1)}, s32[384]{0:T(512)}, u32[]{:S(2)}) copy-start(s32[384]{0:T(512)} %param.11) | copy-start | bytes 4612
  68.6 265.4 %all-to-all-start.1 = ((f32[128,128,128]{2,1,0:T(8,128)}), f32[128,128,128]{2,1,0:T(8,128)}, u32[]{:S(2)}, u32[]{:S(2)}) async-start(f32[128,128,128]{2,1,0:T(8,128)} %scatter_fusion), calls=%async_computation.1 | async-start | bytes 16777216 | tf_op jit(solution)/shard_map/all_to_all | solution.py:37
  349.0 49.9 %copy-start.3 = (s32[64]{0:T(128)S(1)}, s32[64]{0:T(128)}, u32[]{:S(2)}) copy-start(s32[64]{0:T(128)} %param.8) | copy-start | bytes 772
  349.0 237.9 %all-to-all-start.3 = ((bf16[64,128,384]{1,2,0:T(8,128)(2,1)}), bf16[64,128,384]{1,2,0:T(8,128)(2,1)}, u32[]{:S(2)}, u32[]{:S(2)}) async-start(bf16[64,128,384]{1,2,0:T(8,128)(2,1)} %stack.2), calls=%async_computation.3 | async-start | bytes 12582912 | tf_op jit(solution)/shard_map/all_to_all | solution.py:53
  599.2 2.4 copy-start.2
  606.1 43.1 %all-to-all-start.4 = ((bf16[64,2,256]{2,1,0:T(2,128)(2,1)}), bf16[64,2,256]{2,1,0:T(2,128)(2,1)S(1)}, u32[]{:S(2)}, u32[]{:S(2)}) async-start(bf16[64,2,256]{2,1,0:T(2,128)(2,1)} %convert_element_type.30), calls=%async_computation.4 | async-start | bytes 131072 | tf_op jit(solution)/shard_map/all_to_all | solution.py:67
Sparse Core Ops, SparseCore 0:
  10.1 37.0 all-gather.1
